TPU v7x, 32 devices: a whole 2x2x4 slice. The times are simulated.
32 devices in a mesh: grp: 2 (over y), seq: 4 (over z), fsdp: 2 (over x), head: 2 (over core).
Axes of the slice: x: 2, y: 2, z: 4, core: 2. Of those that a mesh axis runs over, the one named last changes fastest.
Arguments:
- tokens: bfloat16 [6144, 3072], P(('grp', 'seq'), 'head'), parts along dimension 0
- qkv_weight: bfloat16 [3072, 1536], P('fsdp', 'head'), may hold values from -0.109375 to 0.109375
- shift_mod: float32 [6144], P('grp'), parts along dimension 0, may hold values from -3 to 3
- scale_mod: float32 [6144], P('grp'), parts along dimension 0, may hold values from -2 to 2
- q_gain: float32 [4, 128], P(('fsdp', 'head'))
- k_gain: float32 [4, 128], P(('fsdp', 'head'))
- cached: bfloat16 [6144, 512], P(('grp', 'seq'), ('fsdp', 'head')), parts along dimension 0, may hold values from -6 to 6
- active: int32 [48], P(('grp', 'seq')), parts along dimension 0, may hold values from -1 to 5, as said below
- cache_slot: int32 [48], P(('grp', 'seq')), parts along dimension 0, may hold values from 0 to 5, as said below
Outputs:
- blended: bfloat16 [6144, 512], P(('grp', 'seq'), ('fsdp', 'head')), parts along dimension 0
There are 2 independent parts, one for each index of `grp`. A program takes and returns all parts, laid end to end along the dimension named above; an argument that names none is the same for every part. Nothing has to cross between parts.
Inputs may be any that keep to these rules, and one draw needn't show every extreme that they name: Entries s * 6 to s * 6 + 5 list the active local blocks of index s of seq in rising order, each at most once, followed by -1 for the rest. Over the whole sequence exactly 12 blocks are active; some index of seq has all 6 blocks active and some has none. `cache_slot`: entries s * 6 to s * 6 + 5 are a permutation of 0 to 5.
All inputs are finite; a program needn't handle non-finite values.
Results may differ from a plain program's by a relative error of at most 0.012.
The roundings to bfloat16 on the way count: a program that leaves them out, or rounds other values in their place, can miss the bound.
Values may be sent and summed in bfloat16 or wider, within the bound.
No kernel may reach another device: no remote copies, remote signals or barrier semaphores. Data moves between devices by JAX's collectives and lax.ppermute only.
A program may use at most 64 MiB of HBM per device.

v0:
```python
import jax
import jax.numpy as jnp
from jax import lax
from jax.sharding import PartitionSpec as P

eps_norm = 1e-06


def rms_scaled(vector, gain_row):
    return (
        vector * lax.rsqrt(jnp.mean(vector * vector, axis=-1, keepdims=True) + eps_norm) * gain_row
    )


def attend_span(carry_state, queries, key_rows, value_rows):
    maxima, totals, accumulated = carry_state
    score_scale = key_rows.shape[1] ** (-0.5)
    scores = (
        jnp.einsum("qd,kd->qk", queries, key_rows, preferred_element_type=jnp.float32) * score_scale
    )
    new_max = jnp.maximum(maxima, jnp.max(scores, axis=1))
    weights = jnp.exp(scores - new_max[:, None])
    shrink = jnp.exp(maxima - new_max)
    totals = totals * shrink + jnp.sum(weights, axis=1)
    accumulated = accumulated * shrink[:, None] + jnp.dot(
        weights.astype(jnp.bfloat16), value_rows, preferred_element_type=jnp.float32
    )
    return (new_max, totals, accumulated)


def attend_keys(carry_state, queries, key_rows, value_rows):
    row_count = key_rows.shape[0]

    def block_step(block_index, journey):
        start_row = block_index * 512
        key_part = lax.dynamic_slice_in_dim(key_rows, start_row, 512, 0)
        value_part = lax.dynamic_slice_in_dim(value_rows, start_row, 512, 0)
        return attend_span(journey, queries, key_part, value_part)

    return lax.fori_loop(0, row_count // 512, block_step, carry_state)


def per_device(
    tokens, qkv_weight, shift_mod, scale_mod, q_gain, k_gain, cached, active, cache_slot
):
    gathered = lax.all_gather(tokens, "head", axis=1, tiled=True).astype(jnp.float32)
    row_mean = jnp.mean(gathered, axis=1, keepdims=True)
    centred = gathered - row_mean
    row_var = jnp.mean(centred * centred, axis=1, keepdims=True)
    normed = (centred * lax.rsqrt(row_var + eps_norm) * (1.0 + scale_mod) + shift_mod).astype(
        jnp.bfloat16
    )
    columns = lax.all_to_all(qkv_weight, "fsdp", split_axis=1, concat_axis=0, tiled=True)
    head_dim = columns.shape[1] // 3
    projected = jnp.dot(normed, columns, preferred_element_type=jnp.float32)
    queries = rms_scaled(projected[:, :head_dim], q_gain).astype(jnp.bfloat16)
    key_rows = rms_scaled(projected[:, head_dim : 2 * head_dim], k_gain).astype(jnp.bfloat16)
    values = projected[:, 2 * head_dim :].astype(jnp.bfloat16)
    tok_rows = tokens.shape[0]
    blocks = active.shape[0]
    block_rows = tok_rows // blocks
    query_blocks = queries.reshape(blocks, block_rows, head_dim)
    slot_ids = jnp.where(active >= 0, active, 0)
    chosen = jnp.take(query_blocks, slot_ids, axis=0).reshape(blocks * block_rows, head_dim)
    query_count = chosen.shape[0]
    start_state = (
        jnp.full((query_count,), -1e30, jnp.float32),
        jnp.zeros((query_count,), jnp.float32),
        jnp.zeros((query_count, head_dim), jnp.float32),
    )
    maxima, totals, accumulated = attend_keys(
        start_state,
        chosen,
        lax.all_gather(key_rows, "seq", axis=0, tiled=True),
        lax.all_gather(values, "seq", axis=0, tiled=True),
    )
    attended = (accumulated / totals[:, None]).astype(jnp.bfloat16)
    slot_rows = attended.reshape(blocks, block_rows, head_dim)
    local_ids = jnp.arange(blocks, dtype=jnp.int32)
    hit_mask = active[None, :] == local_ids[:, None]
    taken = jnp.any(hit_mask, axis=1)
    position = jnp.sum(jnp.where(hit_mask, local_ids[None, :], 0), axis=1)
    fresh_rows = jnp.take(slot_rows, position, axis=0)
    stale_rows = jnp.take(cached.reshape(blocks, block_rows, head_dim), cache_slot, axis=0)
    blended = jnp.where(taken[:, None, None], fresh_rows, stale_rows)
    return blended.reshape(tok_rows, head_dim)


def solution(mesh):
    in_specs = (
        P(("grp", "seq"), "head"),
        P("fsdp", "head"),
        P("grp"),
        P("grp"),
        P(("fsdp", "head"), None),
        P(("fsdp", "head"), None),
        P(("grp", "seq"), ("fsdp", "head")),
        P(("grp", "seq")),
        P(("grp", "seq")),
    )
    out_specs = P(("grp", "seq"), ("fsdp", "head"))
    return jax.shard_map(
        per_device, mesh=mesh, in_specs=in_specs, out_specs=out_specs, check_vma=False
    )
```

profile of v0, /device:TPU:0, one launch (start us, length us, event | category | flops | bytes accessed | tf_op | source)
XLA Modules:
  0.0 116.9 jit_solution(1242417644816890714)
XLA Ops:
  6.5 0.7 all-gather.2.cloned.1.call-update
  7.3 1.0 copy-done.2
  8.2 2.5 %copy.12 = bf16[1536,768]{0,1:T(8,128)(2,1)} copy(bf16[1536,768]{1,0:T(8,128)(2,1)S(1)} %copy-done.2) | data formatting | bytes 4718592 | tf_op args[1]
  10.8 5.1 %all-to-all-start = ((bf16[1536,2,384]{0,2,1:T(8,128)(2,1)}), bf16[1536,2,384]{0,2,1:T(8,128)(2,1)}, u32[]{:S(2)}, u32[]{:S(2)}) async-start(bf16[1536,2,384]{0,2,1:T(8,128)(2,1)} %bitcast), calls=%async_computation | async-start | bytes 4718592 | tf_op jit(solution)/shard_map/all_to_all | solution.py:53
  15.9 0.6 gather_fusion.2
  16.8 28.2 %all-to-all-done = bf16[1536,2,384]{0,2,1:T(8,128)(2,1)} async-done(((bf16[1536,2,384]{0,2,1:T(8,128)(2,1)}), bf16[1536,2,384]{0,2,1:T(8,128)(2,1)}, u32[]{:S(2)}, u32[]{:S(2)}) %all-to-all-start) | async-done | bytes 2359328 | tf_op jit(solution)/shard_map/all_to_all | solution.py:53
  45.0 3.0 %copy.13 = bf16[2,1536,384]{2,1,0:T(8,128)(2,1)S(1)} copy(bf16[2,1536,384]{1,2,0:T(8,128)(2,1)} %bitcast.1) | data formatting | bytes 4718592 | tf_op jit(solution)/shard_map/all_to_all | solution.py:53
  48.1 3.2 %convert_reduce_fusion = f32[768]{0:T(1024)S(1)} fusion(bf16[768,3072]{1,0:T(8,128)(2,1)} %all-gather.2.cloned.1.call-done), kind=kLoop, calls=%fused_computation.19 | loop fusion | flops 4717824 | bytes 4721664 | tf_op jit(solution)/shard_map/reduce_sum | solution.py:47
  51.3 0.6 copy-done.1
  51.9 1.4 %fusion.11 = f32[768]{0:T(1024)S(1)} fusion(bf16[768,3072]{1,0:T(8,128)(2,1)S(1)} %copy-done.1, f32[768]{0:T(1024)S(1)} %broadcast_multiply_fusion), kind=kLoop, calls=%fused_computation.22 | loop fusion | flops 9436416 | bytes 4724736 | tf_op jit(solution)/shard_map/reduce_sum | solution.py:49
  53.3 2.7 %fusion.15 = f32[768,384]{1,0:T(8,128)S(1)} fusion(bf16[3072,384]{1,0:T(8,128)(2,1)S(1)} %bitcast.16, bf16[768,3072]{1,0:T(8,128)(2,1)S(1)} %copy-done.1, f32[3072]{0:T(1024)S(1)} %copy-done.7, f32[3072]{0:T(1024)S(1)} %broadcast_add_fusion, f32[768]{0:T(1024)S(1)} %add_rsqrt_fusion.2, f32[768]{0:T(1024)S(1)} %broadcast_multiply_fusion), kind=kOutput, calls=%fused_computation.26 | convolution fusion | flops 1826095104 | bytes 8288256 | tf_op jit(solution)/shard_map/dot_general | solution.py:55
  56.0 0.3 multiply_reduce_fusion
  56.3 0.3 multiply_convert_fusion
  56.6 20.1 %all_gather.10 = bf16[3072,128]{1,0:T(8,128)(2,1)S(1)} all-gather(bf16[768,128]{1,0:T(8,128)(2,1)S(1)} %get-tuple-element.180), channel_id=1, replica_groups=mesh['grp'=2,'seq'=4,'fsdp'=2,'head'=2] {'seq'}, dimensions={0}, use_global_device_ids=true | all-gather | bytes 983040 | tf_op jit(solution)/shard_map/all_gather | solution.py:74
  76.7 18.1 %all_gather.11 = bf16[3072,128]{1,0:T(8,128)(2,1)} all-gather(bf16[768,128]{1,0:T(8,128)(2,1)S(1)} %slice.27), channel_id=1, replica_groups=mesh['grp'=2,'seq'=4,'fsdp'=2,'head'=2] {'seq'}, dimensions={0}, use_global_device_ids=true | all-gather | bytes 983040 | tf_op jit(solution)/shard_map/all_gather | solution.py:75
  94.8 0.6 gather_fusion
  95.5 12.9 %while.18 = (s32[]{:T(128)}, f32[768]{0:T(1024)S(1)}, f32[768]{0:T(1024)S(1)}, f32[768,128]{1,0:T(8,128)S(1)}, bf16[3072,128]{1,0:T(8,128)(2,1)S(1)}, /*index=5*...) while((s32[]{:T(128)}, f32[768]{0:T(1024)S(1)}, ...), condition=%wide.region_8.10_spmd.clone, body=%wide.region_5.9_spmd.clone.sunk | while | flops 203984640 | bytes 6013111 | solution.py:40
  95.5 0.4 fusion.34
  96.2 1.4 %convolution_add_fusion.2 = f32[768,128]{1,0:T(8,128)S(1)} fusion(f32[512,768]{1,0:T(8,128)S(1)} %get-tuple-element.233, f32[768]{0:T(1024)S(1)} %select_maximum_fusion.2, f32[768,128]{1,0:T(8,128)S(1)} %get-tuple-element.250, f32[768]{0:T(1024)S(1)} %get-tuple-element.235, pred[]{:T(512)S(6)} %compare.3, bf16[3072,128]{1,0:T(8,128)(2,1)} %get-tuple-element.264, ...), kind=kOutput, calls=%fused_computation.7.clone.1 | convolution fusion | flops 101744640 | bytes 2496517 | tf_op jit(solution)/shard_map/while/body/eval_jaxpr/dot_general | solution.py:25
  97.7 0.4 fusion.34
  98.1 0.3 fusion.35
  98.4 1.4 %convolution_add_fusion.2 = f32[768,128]{1,0:T(8,128)S(1)} fusion(f32[512,768]{1,0:T(8,128)S(1)} %get-tuple-element.233, f32[768]{0:T(1024)S(1)} %select_maximum_fusion.2, f32[768,128]{1,0:T(8,128)S(1)} %get-tuple-element.250, f32[768]{0:T(1024)S(1)} %get-tuple-element.235, pred[]{:T(512)S(6)} %compare.3, bf16[3072,128]{1,0:T(8,128)(2,1)} %get-tuple-element.264, ...), kind=kOutput, calls=%fused_computation.7.clone.1 | convolution fusion | flops 101744640 | bytes 2496517 | tf_op jit(solution)/shard_map/while/body/eval_jaxpr/dot_general | solution.py:25
  99.8 0.4 fusion.34
  100.5 1.4 %convolution_add_fusion.2 = f32[768,128]{1,0:T(8,128)S(1)} fusion(f32[512,768]{1,0:T(8,128)S(1)} %get-tuple-element.233, f32[768]{0:T(1024)S(1)} %select_maximum_fusion.2, f32[768,128]{1,0:T(8,128)S(1)} %get-tuple-element.250, f32[768]{0:T(1024)S(1)} %get-tuple-element.235, pred[]{:T(512)S(6)} %compare.3, bf16[3072,128]{1,0:T(8,128)(2,1)} %get-tuple-element.264, ...), kind=kOutput, calls=%fused_computation.7.clone.1 | convolution fusion | flops 101744640 | bytes 2496517 | tf_op jit(solution)/shard_map/while/body/eval_jaxpr/dot_general | solution.py:25
  102.0 0.4 fusion.34
  102.7 1.4 %convolution_add_fusion.2 = f32[768,128]{1,0:T(8,128)S(1)} fusion(f32[512,768]{1,0:T(8,128)S(1)} %get-tuple-element.233, f32[768]{0:T(1024)S(1)} %select_maximum_fusion.2, f32[768,128]{1,0:T(8,128)S(1)} %get-tuple-element.250, f32[768]{0:T(1024)S(1)} %get-tuple-element.235, pred[]{:T(512)S(6)} %compare.3, bf16[3072,128]{1,0:T(8,128)(2,1)} %get-tuple-element.264, ...), kind=kOutput, calls=%fused_computation.7.clone.1 | convolution fusion | flops 101744640 | bytes 2496517 | tf_op jit(solution)/shard_map/while/body/eval_jaxpr/dot_general | solution.py:25
  104.2 0.4 fusion.34
  104.8 1.4 %convolution_add_fusion.2 = f32[768,128]{1,0:T(8,128)S(1)} fusion(f32[512,768]{1,0:T(8,128)S(1)} %get-tuple-element.233, f32[768]{0:T(1024)S(1)} %select_maximum_fusion.2, f32[768,128]{1,0:T(8,128)S(1)} %get-tuple-element.250, f32[768]{0:T(1024)S(1)} %get-tuple-element.235, pred[]{:T(512)S(6)} %compare.3, bf16[3072,128]{1,0:T(8,128)(2,1)} %get-tuple-element.264, ...), kind=kOutput, calls=%fused_computation.7.clone.1 | convolution fusion | flops 101744640 | bytes 2496517 | tf_op jit(solution)/shard_map/while/body/eval_jaxpr/dot_general | solution.py:25
  106.3 0.4 fusion.34
  107.0 1.4 %convolution_add_fusion.2 = f32[768,128]{1,0:T(8,128)S(1)} fusion(f32[512,768]{1,0:T(8,128)S(1)} %get-tuple-element.233, f32[768]{0:T(1024)S(1)} %select_maximum_fusion.2, f32[768,128]{1,0:T(8,128)S(1)} %get-tuple-element.250, f32[768]{0:T(1024)S(1)} %get-tuple-element.235, pred[]{:T(512)S(6)} %compare.3, bf16[3072,128]{1,0:T(8,128)(2,1)} %get-tuple-element.264, ...), kind=kOutput, calls=%fused_computation.7.clone.1 | convolution fusion | flops 101744640 | bytes 2496517 | tf_op jit(solution)/shard_map/while/body/eval_jaxpr/dot_general | solution.py:25
  108.6 0.6 gather_fusion.1
  109.2 0.8 select_select_fusion
  (60 shorter events, 2.1 us)
Async XLA Ops:
  6.5 9.4 %copy-start = (bf16[768,128]{1,0:T(8,128)(2,1)S(1)}, bf16[768,128]{1,0:T(8,128)(2,1)}, u32[]{:S(2)}) copy-start(bf16[768,128]{1,0:T(8,128)(2,1)} %param.19) | copy-start | bytes 589828
  6.5 1.7 %copy-start.2 = (bf16[1536,768]{1,0:T(8,128)(2,1)S(1)}, bf16[1536,768]{1,0:T(8,128)(2,1)}, u32[]{:S(2)}) copy-start(bf16[1536,768]{1,0:T(8,128)(2,1)} %param.14) | copy-start | bytes 7077892
  6.5 41.5 %all-gather.2.cloned.1.call-start = ((), (), s32[]{:S(2)}) async-start(), calls=%async_computation.1 | async-start | bytes 7077888 | tf_op jit(solution)/shard_map/all_gather | solution.py:46
  10.8 5.1 %copy-start.6 = (s32[6]{0:T(128)S(1)}, s32[6]{0:T(128)}, u32[]{:S(2)}) copy-start(s32[6]{0:T(128)} %param.21) | copy-start | bytes 76
  10.8 5.8 %copy-start.8 = (s32[6]{0:T(128)S(1)}, s32[6]{0:T(128)}, u32[]{:S(2)}) copy-start(s32[6]{0:T(128)} %param.20) | copy-start | bytes 76
  10.8 6.1 %copy-start.3 = (f32[3072]{0:T(1024)S(1)}, f32[3072]{0:T(1024)}, u32[]{:S(2)}) copy-start(f32[3072]{0:T(1024)} %param.16) | copy-start | bytes 36868
  10.8 34.3 %all-to-all-start = ((bf16[1536,2,384]{0,2,1:T(8,128)(2,1)}), bf16[1536,2,384]{0,2,1:T(8,128)(2,1)}, u32[]{:S(2)}, u32[]{:S(2)}) async-start(bf16[1536,2,384]{0,2,1:T(8,128)(2,1)} %bitcast), calls=%async_computation | async-start | bytes 4718592 | tf_op jit(solution)/shard_map/all_to_all | solution.py:53
  48.1 3.8 %copy-start.1 = (bf16[768,3072]{1,0:T(8,128)(2,1)S(1)}, bf16[768,3072]{1,0:T(8,128)(2,1)}, u32[]{:S(2)}) copy-start(bf16[768,3072]{1,0:T(8,128)(2,1)} %all-gather.2.cloned.1.call-done) | copy-start | bytes 14155780
  51.9 1.4 %copy-start.7 = (f32[3072]{0:T(1024)S(1)}, f32[3072]{0:T(1024)}, u32[]{:S(2)}) copy-start(f32[3072]{0:T(1024)} %param.15) | copy-start | bytes 36868
  53.2 3.1 %copy-start.4 = (f32[1,128]{1,0:T(1,128)S(1)}, f32[1,128]{1,0:T(1,128)}, u32[]{:S(2)}) copy-start(f32[1,128]{1,0:T(1,128)} %param.17) | copy-start | bytes 1540
  53.2 3.1 %copy-start.5 = (f32[1,128]{1,0:T(1,128)S(1)}, f32[1,128]{1,0:T(1,128)}, u32[]{:S(2)}) copy-start(f32[1,128]{1,0:T(1,128)} %param.18) | copy-start | bytes 1540
Sparse Core Ops, SparseCore 0:
  8.9 17.1 all-gather.1
where the time goes:
time: 117 us
  blocking collectives  38.2 us (33%)
  waiting for transfers between devices  28.9 us (25%)
  matrix products  13.7 us (12%)
  between operations  13.6 us (12%)
  local copies, waits for them, and re-layouts  8.9 us (8%)
  other arithmetic  8.08 us (7%)
  starting transfers between devices  5.07 us (4%)
    all_to_all x1, waiting for transfers between devices, per_device(): lax.all_to_all(qkv_weight, 'fsdp', split_axis=1, concat_axis=0, tiled=True)  28.2 us
    all_gather x1, blocking collectives, per_device(): lax.all_gather(key_rows, 'seq', axis=0, tiled=True)  20.1 us
    all_gather x1, blocking collectives, per_device(): lax.all_gather(values, 'seq', axis=0, tiled=True)  18.1 us
    dot_general x6, matrix products, attend_span(): jnp.dot(weights.astype(jnp.bfloat16), value_rows, preferred_element_type=...  8.68 us
    all_to_all x1, starting transfers between devices, per_device(): lax.all_to_all(qkv_weight, 'fsdp', split_axis=1, concat_axis=0, tiled=True)  5.07 us
    unnamed x19, local copies, waits for them, and re-layouts  4.09 us
    reduce_sum x1, other arithmetic, per_device(): row_mean = jnp.mean(gathered, axis=1, keepdims=True)  3.17 us
    all_to_all x1, local copies, waits for them, and re-layouts, per_device(): lax.all_to_all(qkv_weight, 'fsdp', split_axis=1, concat_axis=0, tiled=True)  3.02 us
  transfers between devices with their start and end apart: 2, of which 1 were waited for; matrix products, arithmetic and copies ran while one was open for 5% of the time, Pallas kernels for 0%

commit v1 on v0

--- a/solution.py
+++ b/solution.py
@@ -50,7 +50,12 @@
     normed = (centred * lax.rsqrt(row_var + eps_norm) * (1.0 + scale_mod) + shift_mod).astype(
         jnp.bfloat16
     )
-    columns = lax.all_to_all(qkv_weight, "fsdp", split_axis=1, concat_axis=0, tiled=True)
+    columns = jnp.concatenate(
+        lax.all_to_all(
+            jnp.stack(jnp.split(qkv_weight, lax.axis_size("fsdp"), axis=1)), "fsdp", 0, 0
+        ),
+        axis=0,
+    )
     head_dim = columns.shape[1] // 3
     projected = jnp.dot(normed, columns, preferred_element_type=jnp.float32)
     queries = rms_scaled(projected[:, :head_dim], q_gain).astype(jnp.bfloat16)

time: 117 us -> 109 us (0.932)
  waiting for transfers between devices: 28.9 us -> 23.3 us
  local copies, waits for them, and re-layouts: 8.9 us -> 3.61 us
  matrix products: 13.7 us -> 15.7 us
  other arithmetic: 8.08 us -> 9.79 us
    all_to_all x1, waiting for transfers between devices: 28.2 us -> 12.1 us  [per_device(): lax.all_to_all(jnp.stack(jnp.split(qkv_weight, lax.axis_size('fsdp'), axi...]
    all_gather x1, waiting for transfers between devices: 0.02 us -> 10.6 us  [per_device(): lax.all_gather(tokens, 'head', axis=1, tiled=True).astype(jnp.float32)]
    all_to_all x1 -> x0, local copies, waits for them, and re-layouts: 3.02 us -> none  [per_device(): lax.all_to_all(qkv_weight, 'fsdp', split_axis=1, concat_axis=0, tiled=True)]
    unnamed x19 -> x18, local copies, waits for them, and re-layouts: 4.09 us -> 1.58 us
    dot_general x1, matrix products: 2.73 us -> 4.76 us  [per_device(): projected = jnp.dot(normed, columns, preferred_element_type=jnp.float32)]
    another operation x0 -> x1, other arithmetic: none -> 1.71 us  [per_device(): jnp.stack(jnp.split(qkv_weight, lax.axis_size('fsdp'), axis=1))]
  transfers between devices with their start and end apart: 2 -> 2, of which waited for: 1 -> 2; matrix products, arithmetic and copies ran while one was open for 5% -> 7% of each run, Pallas kernels for 0% -> 0%
where the time goes in v1:
time: 109 us
  blocking collectives  38.2 us (35%)
  waiting for transfers between devices  23.3 us (21%)
  matrix products  15.7 us (14%)
  between operations  13.6 us (12%)
  other arithmetic  9.79 us (9%)
  starting transfers between devices  4.37 us (4%)
  local copies, waits for them, and re-layouts  3.61 us (3%)
    all_gather x1, blocking collectives, per_device(): lax.all_gather(key_rows, 'seq', axis=0, tiled=True)  20.1 us
    all_gather x1, blocking collectives, per_device(): lax.all_gather(values, 'seq', axis=0, tiled=True)  18.1 us
    all_to_all x1, waiting for transfers between devices, per_device(): lax.all_to_all(jnp.stack(jnp.split(qkv_weight, lax.axis_size('fsdp'), axi...  12.1 us
    all_gather x1, waiting for transfers between devices, per_device(): lax.all_gather(tokens, 'head', axis=1, tiled=True).astype(jnp.float32)  10.6 us
    dot_general x6, matrix products, attend_span(): jnp.dot(weights.astype(jnp.bfloat16), value_rows, preferred_element_type=...  8.68 us
    dot_general x1, matrix products, per_device(): projected = jnp.dot(normed, columns, preferred_element_type=jnp.float32)  4.76 us
    all_to_all x1, starting transfers between devices, per_device(): lax.all_to_all(jnp.stack(jnp.split(qkv_weight, lax.axis_size('fsdp'), axi...  4.37 us
    reduce_sum x1, other arithmetic, per_device(): row_mean = jnp.mean(gathered, axis=1, keepdims=True)  3.17 us
  transfers between devices with their start and end apart: 2, of which 2 were waited for; matrix products, arithmetic and copies ran while one was open for 7% of the time, Pallas kernels for 0%

profile of v1, /device:TPU:0, one launch (start us, length us, event | category | flops | bytes accessed | tf_op | source)
XLA Modules:
  0.0 108.9 jit_solution(11883256424376087553)
XLA Ops:
  6.5 0.7 all-gather.2.cloned.1.call-update
  7.3 1.0 copy-done.2
  8.5 1.7 %pad_maximum_fusion = bf16[2,1536,384]{2,1,0:T(8,128)(2,1)} fusion(bf16[1,1536,384]{2,1,0:T(8,128)(2,1)S(1)} %get-tuple-element.180, bf16[1,1536,384]{2,1,0:T(8,128)(2,1)S(1)} %get-tuple-element.179), kind=kLoop, calls=%fused_computation.31 | loop fusion | flops 1179648 | bytes 4718592 | tf_op jit(solution)/shard_map/stack | solution.py:55
  10.2 4.4 %all-to-all-start = ((bf16[2,1536,384]{2,1,0:T(8,128)(2,1)}), bf16[2,1536,384]{2,1,0:T(8,128)(2,1)S(1)}, u32[]{:S(2)}, u32[]{:S(2)}) async-start(bf16[2,1536,384]{2,1,0:T(8,128)(2,1)} %pad_maximum_fusion), calls=%async_computation | async-start | bytes 4718592 | tf_op jit(solution)/shard_map/all_to_all | solution.py:54
  14.6 0.6 gather_fusion.2
  15.5 10.6 %all-gather.2.cloned.1.call-done = bf16[768,3072]{1,0:T(8,128)(2,1)} async-done(((bf16[768,1536]{1,0:T(8,128)(2,1)}), bf16[768,3072]{1,0:T(8,128)(2,1)}) %all-gather.2.cloned.1.call-update) | async-done | bytes 4718608 | tf_op jit(solution)/shard_map/all_gather | solution.py:46
  26.1 3.2 %convert_reduce_fusion = f32[768]{0:T(1024)S(1)} fusion(bf16[768,3072]{1,0:T(8,128)(2,1)} %all-gather.2.cloned.1.call-done), kind=kLoop, calls=%fused_computation.19 | loop fusion | flops 4717824 | bytes 4721664 | tf_op jit(solution)/shard_map/reduce_sum | solution.py:47
  29.3 0.6 copy-done.1
  29.8 1.4 %fusion.11 = f32[768]{0:T(1024)S(1)} fusion(bf16[768,3072]{1,0:T(8,128)(2,1)S(1)} %copy-done.1, f32[768]{0:T(1024)S(1)} %broadcast_multiply_fusion), kind=kLoop, calls=%fused_computation.22 | loop fusion | flops 9436416 | bytes 4724736 | tf_op jit(solution)/shard_map/reduce_sum | solution.py:49
  31.2 12.1 %all-to-all-done = bf16[2,1536,384]{2,1,0:T(8,128)(2,1)S(1)} async-done(((bf16[2,1536,384]{2,1,0:T(8,128)(2,1)}), bf16[2,1536,384]{2,1,0:T(8,128)(2,1)S(1)}, u32[]{:S(2)}, u32[]{:S(2)}) %all-to-all-start) | async-done | bytes 2359328 | tf_op jit(solution)/shard_map/all_to_all | solution.py:54
  43.3 4.8 %fusion.15 = f32[768,384]{1,0:T(8,128)S(1)} fusion(bf16[3072,384]{1,0:T(8,128)(2,1)S(1)} %bitcast.18, bf16[768,3072]{1,0:T(8,128)(2,1)} %all-gather.2.cloned.1.call-done, f32[3072]{0:T(1024)S(1)} %copy-done.7, f32[3072]{0:T(1024)S(1)} %broadcast_add_fusion, f32[768]{0:T(1024)S(1)} %add_rsqrt_fusion.2, f32[768]{0:T(1024)S(1)} %broadcast_multiply_fusion), kind=kOutput, calls=%fused_computation.26 | convolution fusion | flops 1826095104 | bytes 8288256 | tf_op jit(solution)/shard_map/dot_general | solution.py:60
  48.1 0.3 multiply_reduce_fusion
  48.4 0.3 multiply_convert_fusion
  48.7 20.1 %all_gather.10 = bf16[3072,128]{1,0:T(8,128)(2,1)S(1)} all-gather(bf16[768,128]{1,0:T(8,128)(2,1)S(1)} %get-tuple-element.182), channel_id=1, replica_groups=mesh['grp'=2,'seq'=4,'fsdp'=2,'head'=2] {'seq'}, dimensions={0}, use_global_device_ids=true | all-gather | bytes 983040 | tf_op jit(solution)/shard_map/all_gather | solution.py:79
  68.8 18.1 %all_gather.11 = bf16[3072,128]{1,0:T(8,128)(2,1)} all-gather(bf16[768,128]{1,0:T(8,128)(2,1)S(1)} %slice.27), channel_id=1, replica_groups=mesh['grp'=2,'seq'=4,'fsdp'=2,'head'=2] {'seq'}, dimensions={0}, use_global_device_ids=true | all-gather | bytes 983040 | tf_op jit(solution)/shard_map/all_gather | solution.py:80
  86.9 0.6 gather_fusion
  87.6 12.9 %while.18 = (s32[]{:T(128)}, f32[768]{0:T(1024)S(1)}, f32[768]{0:T(1024)S(1)}, f32[768,128]{1,0:T(8,128)S(1)}, bf16[3072,128]{1,0:T(8,128)(2,1)S(1)}, /*index=5*...) while((s32[]{:T(128)}, f32[768]{0:T(1024)S(1)}, ...), condition=%wide.region_8.10_spmd.clone, body=%wide.region_5.9_spmd.clone.sunk | while | flops 203984640 | bytes 6013111 | solution.py:40
  87.6 0.4 fusion.34
  88.0 0.3 fusion.35
  88.3 1.4 %convolution_add_fusion.2 = f32[768,128]{1,0:T(8,128)S(1)} fusion(f32[512,768]{1,0:T(8,128)S(1)} %get-tuple-element.235, f32[768]{0:T(1024)S(1)} %select_maximum_fusion.2, f32[768,128]{1,0:T(8,128)S(1)} %get-tuple-element.252, f32[768]{0:T(1024)S(1)} %get-tuple-element.237, pred[]{:T(512)S(6)} %compare.3, bf16[3072,128]{1,0:T(8,128)(2,1)} %get-tuple-element.266, ...), kind=kOutput, calls=%fused_computation.7.clone.1 | convolution fusion | flops 101744640 | bytes 2496517 | tf_op jit(solution)/shard_map/while/body/eval_jaxpr/dot_general | solution.py:25
  89.7 0.4 fusion.34
  90.4 1.4 %convolution_add_fusion.2 = f32[768,128]{1,0:T(8,128)S(1)} fusion(f32[512,768]{1,0:T(8,128)S(1)} %get-tuple-element.235, f32[768]{0:T(1024)S(1)} %select_maximum_fusion.2, f32[768,128]{1,0:T(8,128)S(1)} %get-tuple-element.252, f32[768]{0:T(1024)S(1)} %get-tuple-element.237, pred[]{:T(512)S(6)} %compare.3, bf16[3072,128]{1,0:T(8,128)(2,1)} %get-tuple-element.266, ...), kind=kOutput, calls=%fused_computation.7.clone.1 | convolution fusion | flops 101744640 | bytes 2496517 | tf_op jit(solution)/shard_map/while/body/eval_jaxpr/dot_general | solution.py:25
  91.9 0.4 fusion.34
  92.6 1.4 %convolution_add_fusion.2 = f32[768,128]{1,0:T(8,128)S(1)} fusion(f32[512,768]{1,0:T(8,128)S(1)} %get-tuple-element.235, f32[768]{0:T(1024)S(1)} %select_maximum_fusion.2, f32[768,128]{1,0:T(8,128)S(1)} %get-tuple-element.252, f32[768]{0:T(1024)S(1)} %get-tuple-element.237, pred[]{:T(512)S(6)} %compare.3, bf16[3072,128]{1,0:T(8,128)(2,1)} %get-tuple-element.266, ...), kind=kOutput, calls=%fused_computation.7.clone.1 | convolution fusion | flops 101744640 | bytes 2496517 | tf_op jit(solution)/shard_map/while/body/eval_jaxpr/dot_general | solution.py:25
  94.0 0.4 fusion.34
  94.7 1.4 %convolution_add_fusion.2 = f32[768,128]{1,0:T(8,128)S(1)} fusion(f32[512,768]{1,0:T(8,128)S(1)} %get-tuple-element.235, f32[768]{0:T(1024)S(1)} %select_maximum_fusion.2, f32[768,128]{1,0:T(8,128)S(1)} %get-tuple-element.252, f32[768]{0:T(1024)S(1)} %get-tuple-element.237, pred[]{:T(512)S(6)} %compare.3, bf16[3072,128]{1,0:T(8,128)(2,1)} %get-tuple-element.266, ...), kind=kOutput, calls=%fused_computation.7.clone.1 | convolution fusion | flops 101744640 | bytes 2496517 | tf_op jit(solution)/shard_map/while/body/eval_jaxpr/dot_general | solution.py:25
  96.2 0.4 fusion.34
  96.9 1.4 %convolution_add_fusion.2 = f32[768,128]{1,0:T(8,128)S(1)} fusion(f32[512,768]{1,0:T(8,128)S(1)} %get-tuple-element.235, f32[768]{0:T(1024)S(1)} %select_maximum_fusion.2, f32[768,128]{1,0:T(8,128)S(1)} %get-tuple-element.252, f32[768]{0:T(1024)S(1)} %get-tuple-element.237, pred[]{:T(512)S(6)} %compare.3, bf16[3072,128]{1,0:T(8,128)(2,1)} %get-tuple-element.266, ...), kind=kOutput, calls=%fused_computation.7.clone.1 | convolution fusion | flops 101744640 | bytes 2496517 | tf_op jit(solution)/shard_map/while/body/eval_jaxpr/dot_general | solution.py:25
  98.4 0.4 fusion.34
  99.0 1.4 %convolution_add_fusion.2 = f32[768,128]{1,0:T(8,128)S(1)} fusion(f32[512,768]{1,0:T(8,128)S(1)} %get-tuple-element.235, f32[768]{0:T(1024)S(1)} %select_maximum_fusion.2, f32[768,128]{1,0:T(8,128)S(1)} %get-tuple-element.252, f32[768]{0:T(1024)S(1)} %get-tuple-element.237, pred[]{:T(512)S(6)} %compare.3, bf16[3072,128]{1,0:T(8,128)(2,1)} %get-tuple-element.266, ...), kind=kOutput, calls=%fused_computation.7.clone.1 | convolution fusion | flops 101744640 | bytes 2496517 | tf_op jit(solution)/shard_map/while/body/eval_jaxpr/dot_general | solution.py:25
  100.7 0.6 gather_fusion.1
  101.3 0.8 select_select_fusion
  (60 shorter events, 2.3 us)
Async XLA Ops:
  6.5 8.1 %copy-start = (bf16[768,128]{1,0:T(8,128)(2,1)S(1)}, bf16[768,128]{1,0:T(8,128)(2,1)}, u32[]{:S(2)}) copy-start(bf16[768,128]{1,0:T(8,128)(2,1)} %param.19) | copy-start | bytes 589828
  6.5 1.7 %copy-start.2 = (bf16[1536,768]{1,0:T(8,128)(2,1)S(1)}, bf16[1536,768]{1,0:T(8,128)(2,1)}, u32[]{:S(2)}) copy-start(bf16[1536,768]{1,0:T(8,128)(2,1)} %param.14) | copy-start | bytes 7077892
  6.5 19.5 %all-gather.2.cloned.1.call-start = ((), (), s32[]{:S(2)}) async-start(), calls=%async_computation.1 | async-start | bytes 7077888 | tf_op jit(solution)/shard_map/all_gather | solution.py:46
  10.2 4.4 %copy-start.6 = (s32[6]{0:T(128)S(1)}, s32[6]{0:T(128)}, u32[]{:S(2)}) copy-start(s32[6]{0:T(128)} %param.21) | copy-start | bytes 76
  10.2 5.0 %copy-start.8 = (s32[6]{0:T(128)S(1)}, s32[6]{0:T(128)}, u32[]{:S(2)}) copy-start(s32[6]{0:T(128)} %param.20) | copy-start | bytes 76
  10.2 5.3 %copy-start.3 = (f32[3072]{0:T(1024)S(1)}, f32[3072]{0:T(1024)}, u32[]{:S(2)}) copy-start(f32[3072]{0:T(1024)} %param.16) | copy-start | bytes 36868
  10.2 33.1 %all-to-all-start = ((bf16[2,1536,384]{2,1,0:T(8,128)(2,1)}), bf16[2,1536,384]{2,1,0:T(8,128)(2,1)S(1)}, u32[]{:S(2)}, u32[]{:S(2)}) async-start(bf16[2,1536,384]{2,1,0:T(8,128)(2,1)} %pad_maximum_fusion), calls=%async_computation | async-start | bytes 4718592 | tf_op jit(solution)/shard_map/all_to_all | solution.py:54
  26.1 3.8 %copy-start.1 = (bf16[768,3072]{1,0:T(8,128)(2,1)S(1)}, bf16[768,3072]{1,0:T(8,128)(2,1)}, u32[]{:S(2)}) copy-start(bf16[768,3072]{1,0:T(8,128)(2,1)} %all-gather.2.cloned.1.call-done) | copy-start | bytes 14155780
  29.8 13.4 %copy-start.7 = (f32[3072]{0:T(1024)S(1)}, f32[3072]{0:T(1024)}, u32[]{:S(2)}) copy-start(f32[3072]{0:T(1024)} %param.15) | copy-start | bytes 36868
  43.3 5.1 %copy-start.4 = (f32[1,128]{1,0:T(1,128)S(1)}, f32[1,128]{1,0:T(1,128)}, u32[]{:S(2)}) copy-start(f32[1,128]{1,0:T(1,128)} %param.17) | copy-start | bytes 1540
  43.3 5.1 %copy-start.5 = (f32[1,128]{1,0:T(1,128)S(1)}, f32[1,128]{1,0:T(1,128)}, u32[]{:S(2)}) copy-start(f32[1,128]{1,0:T(1,128)} %param.18) | copy-start | bytes 1540
Sparse Core Ops, SparseCore 0:
  8.9 17.1 all-gather.1
